TPU v7x, 32 devices: a whole 2x2x4 slice. The times are simulated.
32 devices in a mesh: rep: 4 (over y, x), shard: 8 (over z, core).
Axes of the slice: x: 2, y: 2, z: 4, core: 2. Of those that a mesh axis runs over, the one named last changes fastest.
Arguments:
- inputs: bfloat16 [32768, 1024], P(('rep', 'shard')), may hold values from -6 to 6
- query_weight: bfloat16 [1024, 256], P('shard'), may hold values from -0.1875 to 0.1875
- key_weight: bfloat16 [1024, 256], P('shard'), may hold values from -0.1875 to 0.1875
- value_weight: bfloat16 [1024, 1024], P('shard'), may hold values from -0.1875 to 0.1875
- out_weight: bfloat16 [1024, 1024], P('shard'), may hold values from -6 to 6
- gate_weight: bfloat16 [1024, 2752], P('shard'), may hold values from -0.1875 to 0.1875
- up_weight: bfloat16 [1024, 2752], P('shard'), may hold values from -0.1875 to 0.1875
- down_weight: bfloat16 [1024, 2752], P('shard'), may hold values from -0.109375 to 0.109375
- attn_gain: bfloat16 [1024], P('shard'), may hold values from 0.25 to 1.75
- mlp_gain: bfloat16 [1024], P('shard'), may hold values from 0.25 to 1.75
- slot_of: int32 [4, 8], P('rep'), may hold values from 0 to 7, each once within a row
- parent_of: int32 [4, 8], P('rep'), may hold values from 0 to 1, as said below
- cotangent: bfloat16 [32768, 1024], P(('rep', 'shard')), may hold values from -6 to 6
Outputs:
- block_out: bfloat16 [32768, 1024], P(('rep', 'shard'))
- input_grad: float32 [32768, 1024], P(('rep', 'shard'))
- query_grad: float32 [1024, 256], P('shard')
- key_grad: float32 [1024, 256], P('shard')
- value_grad: float32 [1024, 1024], P('shard')
- out_grad: float32 [1024, 1024], P('shard')
- gate_grad: float32 [1024, 2752], P('shard')
- up_grad: float32 [1024, 2752], P('shard')
- down_grad: float32 [1024, 2752], P('shard')
- attn_gain_grad: float32 [1024], P('shard')
- mlp_gain_grad: float32 [1024], P('shard')
Inputs may be any that keep to these rules, and one draw needn't show every extreme that they name: `slot_of`: each row is a permutation of the slots of its group. `parent_of`: each row names each of the 2 families for exactly 4 continuations.
All inputs are finite; a program needn't handle non-finite values.
Results may differ from a plain program's by a relative error of at most 0.02.
Values may be sent and summed in bfloat16 or wider, within the bound.
No kernel may reach another device: no remote copies, remote signals or barrier semaphores. Data moves between devices by JAX's collectives and lax.ppermute only.
A program may use at most 320 MiB of HBM per device.

v0:
```python
from functools import partial
import math

import jax
import jax.numpy as jnp
from jax import lax
from jax.sharding import PartitionSpec as P

HEADS = 16
CONT_PER = 4


norm_eps = 1e-05


def on_whole(value, axis, dim, block):
    whole = lax.all_gather(value, axis, axis=dim, tiled=True)
    return block(whole, jnp.int32(0))


def features(vectors):
    width = vectors.shape[-1]
    square = vectors[..., :, None] * vectors[..., None, :]
    square = square.reshape(vectors.shape[:-1] + (width * width,))
    return jnp.concatenate(
        [
            jnp.ones_like(vectors[..., :1]),
            vectors / width**0.25,
            square / (math.sqrt(2.0) * math.sqrt(width)),
        ],
        axis=-1,
    )


def contract_last(left, right):
    return lax.dot_general(
        left, right, (((1,), (1,)), ((), ())), preferred_element_type=jnp.float32
    )


def contract_first(left, right):
    return lax.dot_general(
        left, right, (((0,), (0,)), ((), ())), preferred_element_type=jnp.float32
    )


def group_heads(values):
    rows_count, heads_count, inner_dim = values.shape
    return values.reshape(rows_count, heads_count // 4, 4, inner_dim).transpose(1, 0, 2, 3)


def group_plain(values):
    rows_count, heads_count = values.shape
    return values.reshape(rows_count, heads_count // 4, 4).transpose(1, 0, 2)


def ungroup_heads(values):
    block_count, rows_count, block_heads, inner_dim = values.shape
    return values.transpose(1, 0, 2, 3).reshape(rows_count, block_count * block_heads, inner_dim)


def ungroup_plain(values):
    block_count, rows_count, block_heads = values.shape
    return values.transpose(1, 0, 2).reshape(rows_count, block_count * block_heads)


def kernel_of(queries, key_heads, allowed):
    scores = jnp.einsum(
        "thf,uhf->htu", queries, key_heads, preferred_element_type=jnp.float32
    ) / math.sqrt(queries.shape[-1])
    kernel = jnp.where(allowed[None], 1.0 + scores + 0.5 * scores * scores, 0.0)
    return (scores, kernel)


def local_forward(allowed, blocks):
    queries, key_heads, value_heads = blocks
    scores, kernel = kernel_of(queries, key_heads, allowed)
    numerator = jnp.einsum(
        "htu,uhe->the", kernel.astype(jnp.bfloat16), value_heads, preferred_element_type=jnp.float32
    )
    denominator = jnp.sum(kernel, axis=2).T
    return (numerator, denominator)


def local_backward(allowed, blocks):
    queries, key_heads, value_heads, grad_num, grad_den = blocks
    scores, kernel = kernel_of(queries, key_heads, allowed)
    grad_kernel = (
        jnp.einsum("the,uhe->htu", grad_num, value_heads, preferred_element_type=jnp.float32)
        + grad_den.T.astype(jnp.float32)[:, :, None]
    )
    grad_scores = (jnp.where(allowed[None], grad_kernel, 0.0) * (1.0 + scores)).astype(jnp.bfloat16)
    root = math.sqrt(queries.shape[-1])
    grad_query = (
        jnp.einsum("htu,uhf->thf", grad_scores, key_heads, preferred_element_type=jnp.float32)
        / root
    )
    grad_key = (
        jnp.einsum("htu,thf->uhf", grad_scores, queries, preferred_element_type=jnp.float32) / root
    )
    grad_value = jnp.einsum(
        "htu,the->uhe", kernel.astype(jnp.bfloat16), grad_num, preferred_element_type=jnp.float32
    )
    return (grad_query, grad_key, grad_value)


def local(
    inputs,
    query_weight,
    key_weight,
    value_weight,
    out_weight,
    gate_weight,
    up_weight,
    down_weight,
    attn_gain,
    mlp_gain,
    slot_of,
    parent_of,
    cotangent,
):
    tok_rows, width = inputs.shape
    half_rows = tok_rows // 2
    qk_width = query_weight.shape[1]
    value_width = value_weight.shape[1]
    hidden_width = gate_weight.shape[1]
    state_rows = value_width + HEADS
    shards = lax.axis_size("shard")
    own_index = lax.axis_index("shard")
    slot_ids = slot_of[0]
    parent_ids = parent_of[0]
    prompt_slots = shards // 2
    pieces_per = CONT_PER // 2
    own_slot = lax.dynamic_index_in_dim(slot_ids, own_index, keepdims=False)
    own_prompt = own_slot < prompt_slots
    source_prompt = slot_ids < prompt_slots
    source_family = slot_ids // pieces_per
    earlier = (
        source_prompt
        & (source_family == own_slot // pieces_per)
        & (slot_ids % pieces_per < own_slot % pieces_per)
    )
    pair_index = jnp.clip(own_slot - prompt_slots, 0, shards // 2 - 1)
    first_parent = lax.dynamic_index_in_dim(parent_ids, 2 * pair_index, keepdims=False)
    second_parent = lax.dynamic_index_in_dim(parent_ids, 2 * pair_index + 1, keepdims=False)
    from_first = source_prompt & (source_family == first_parent)
    from_second = source_prompt & (source_family == second_parent)
    source_mix = jnp.where(
        own_prompt, jnp.stack([earlier, earlier]), jnp.stack([from_first, from_second])
    ).astype(jnp.float32)
    positions = lax.broadcasted_iota(jnp.int32, (tok_rows,), 0)
    segment_ids = jnp.where(own_prompt, 0, positions // half_rows)
    allowed = (positions[None, :] <= positions[:, None]) & (
        segment_ids[None, :] == segment_ids[:, None]
    )
    x_float = inputs.astype(jnp.float32)
    inv_one = lax.rsqrt(jnp.mean(x_float * x_float, axis=1, keepdims=True) + norm_eps)
    norm_one = x_float * inv_one
    part_query = lax.all_gather(query_weight, "shard", axis=0, tiled=True)
    part_key = lax.all_gather(key_weight, "shard", axis=0, tiled=True)
    part_value = lax.all_gather(value_weight, "shard", axis=0, tiled=True)
    part_gain = lax.all_gather(attn_gain, "shard", axis=0, tiled=True)
    scaled = (norm_one * part_gain.astype(jnp.float32)).astype(jnp.bfloat16)
    acc_query = jnp.dot(scaled, part_query, preferred_element_type=jnp.float32)
    acc_key = jnp.dot(scaled, part_key, preferred_element_type=jnp.float32)
    acc_value = jnp.dot(scaled, part_value, preferred_element_type=jnp.float32)
    hidden_one = scaled
    gain_one = part_gain
    queries = acc_query.astype(jnp.bfloat16).reshape(tok_rows, HEADS, -1)
    key_heads = acc_key.astype(jnp.bfloat16).reshape(tok_rows, HEADS, -1)
    value_heads = acc_value.astype(jnp.bfloat16).reshape(tok_rows, HEADS, -1)
    query_float = queries.astype(jnp.float32)
    key_float = key_heads.astype(jnp.float32)
    query_feat = features(query_float).astype(jnp.bfloat16)
    key_feat = features(key_float).astype(jnp.bfloat16)
    taylor = query_feat.shape[2]
    ones_col = jnp.ones((tok_rows,), jnp.bfloat16)
    value_state = jnp.einsum(
        "the,thf->hef", value_heads, key_feat, preferred_element_type=jnp.float32
    ).reshape(value_width, taylor)
    norm_state = jnp.einsum("t,thf->hf", ones_col, key_feat, preferred_element_type=jnp.float32)
    own_state = jnp.concatenate([value_state, norm_state], axis=0).astype(jnp.bfloat16)
    add_portion = lax.all_gather(own_state, "shard", axis=0, tiled=True)
    sources = add_portion.shape[0] // state_rows
    mix = source_mix.astype(jnp.bfloat16)
    slot_states = jnp.einsum(
        "sn,nrf->srf",
        mix,
        add_portion.reshape(sources, state_rows, taylor),
        preferred_element_type=jnp.float32,
    )
    used_states = slot_states.astype(jnp.bfloat16)
    used_values = used_states[:, :value_width].reshape(2, HEADS, -1, taylor)
    used_norms = used_states[:, value_width:]
    halves_query = query_feat.reshape(2, half_rows, HEADS, taylor)
    state_num = jnp.einsum(
        "nthf,nhef->nthe", halves_query, used_values, preferred_element_type=jnp.float32
    ).reshape(tok_rows, HEADS, -1)
    state_den = jnp.einsum(
        "nthf,nhf->nth", halves_query, used_norms, preferred_element_type=jnp.float32
    ).reshape(tok_rows, HEADS)
    local_num, local_den = lax.map(
        partial(local_forward, allowed),
        (group_heads(queries), group_heads(key_heads), group_heads(value_heads)),
    )
    numerator = ungroup_heads(local_num) + state_num
    denominator = ungroup_plain(local_den) + state_den
    ratio = numerator / denominator[:, :, None]
    mixed = ratio.reshape(tok_rows, value_width).astype(jnp.bfloat16)
    attn_out = on_whole(
        out_weight, "shard", 0, lambda portion, offset: contract_last(mixed, portion)
    )
    after_attn = x_float + attn_out
    inv_two = lax.rsqrt(jnp.mean(after_attn * after_attn, axis=1, keepdims=True) + norm_eps)
    norm_two = after_attn * inv_two
    part_gate = lax.all_gather(gate_weight, "shard", axis=0, tiled=True)
    part_up = lax.all_gather(up_weight, "shard", axis=0, tiled=True)
    part_gain = lax.all_gather(mlp_gain, "shard", axis=0, tiled=True)
    scaled = (norm_two * part_gain.astype(jnp.float32)).astype(jnp.bfloat16)
    gate_pre = jnp.dot(scaled, part_gate, preferred_element_type=jnp.float32)
    up_pre = jnp.dot(scaled, part_up, preferred_element_type=jnp.float32)
    sigma = jax.nn.sigmoid(gate_pre)
    activated = (gate_pre * sigma * up_pre).astype(jnp.bfloat16)
    mlp_out = on_whole(
        down_weight, "shard", 0, lambda portion, offset: contract_last(activated, portion)
    )
    block_out = (after_attn + mlp_out).astype(jnp.bfloat16)
    cot_float = cotangent.astype(jnp.float32)
    grad_act = jnp.dot(
        cotangent,
        lax.all_gather(down_weight, "shard", axis=0, tiled=True),
        preferred_element_type=jnp.float32,
    )
    grad_up = (grad_act * gate_pre * sigma).astype(jnp.bfloat16)
    grad_gate = (grad_act * up_pre * sigma * (1.0 + gate_pre * (1.0 - sigma))).astype(jnp.bfloat16)
    grad_hidden_two = on_whole(
        (gate_weight, up_weight),
        "shard",
        0,
        lambda portion, offset: contract_last(grad_gate, portion[0])
        + contract_last(grad_up, portion[1]),
    )
    grad_norm_two = grad_hidden_two * part_gain.astype(jnp.float32)
    grad_after = cot_float + inv_two * (
        grad_norm_two - norm_two * jnp.mean(grad_norm_two * norm_two, axis=1, keepdims=True)
    )
    grad_attn = grad_after.astype(jnp.bfloat16)
    grad_mixed = jnp.dot(
        grad_attn,
        lax.all_gather(out_weight, "shard", axis=0, tiled=True),
        preferred_element_type=jnp.float32,
    ).reshape(tok_rows, HEADS, -1)
    grad_num = (grad_mixed / denominator[:, :, None]).astype(jnp.bfloat16)
    grad_den = (-jnp.sum(grad_mixed * ratio, axis=2) / denominator).astype(jnp.bfloat16)
    local_dq, local_dk, local_dv = lax.map(
        partial(local_backward, allowed),
        (
            group_heads(queries),
            group_heads(key_heads),
            group_heads(value_heads),
            group_heads(grad_num),
            group_plain(grad_den),
        ),
    )
    halves_num = grad_num.reshape(2, half_rows, HEADS, -1)
    halves_den = grad_den.reshape(2, half_rows, HEADS)
    grad_query_feat = (
        jnp.einsum("nthe,nhef->nthf", halves_num, used_values, preferred_element_type=jnp.float32)
        + jnp.einsum("nth,nhf->nthf", halves_den, used_norms, preferred_element_type=jnp.float32)
    ).reshape(tok_rows, HEADS, taylor)
    grad_slot_values = jnp.einsum(
        "nthf,nthe->nhef", halves_query, halves_num, preferred_element_type=jnp.float32
    ).reshape(2, value_width, taylor)
    grad_slot_norms = jnp.einsum(
        "nthf,nth->nhf", halves_query, halves_den, preferred_element_type=jnp.float32
    )
    grad_slots = jnp.concatenate([grad_slot_values, grad_slot_norms], axis=1)
    mix = source_mix
    grad_state = lax.psum_scatter(
        jnp.einsum("sn,srf->nrf", mix, grad_slots, precision=lax.Precision.HIGHEST)
        .reshape(state_rows * lax.axis_size("shard"), taylor)
        .astype(jnp.bfloat16),
        "shard",
        scatter_dimension=0,
        tiled=True,
    )
    grad_value_state = grad_state[:value_width].reshape(HEADS, -1, taylor)
    grad_norm_state = grad_state[value_width:]
    grad_key_feat = (
        jnp.einsum(
            "hef,the->thf", grad_value_state, value_heads, preferred_element_type=jnp.float32
        )
        + grad_norm_state.astype(jnp.float32)[None]
    )
    value_from_state = jnp.einsum(
        "thf,hef->the", key_feat, grad_value_state, preferred_element_type=jnp.float32
    )
    query_from_feat = jax.vjp(features, query_float)[1](grad_query_feat)[0]
    key_from_feat = jax.vjp(features, key_float)[1](grad_key_feat)[0]
    grad_queries = (
        (ungroup_heads(local_dq) + query_from_feat).reshape(tok_rows, qk_width).astype(jnp.bfloat16)
    )
    grad_keys = (
        (ungroup_heads(local_dk) + key_from_feat).reshape(tok_rows, qk_width).astype(jnp.bfloat16)
    )
    grad_values = (
        (ungroup_heads(local_dv) + value_from_state)
        .reshape(tok_rows, value_width)
        .astype(jnp.bfloat16)
    )
    grad_hidden_one = on_whole(
        (query_weight, key_weight, value_weight),
        "shard",
        0,
        lambda portion, offset: contract_last(grad_queries, portion[0])
        + contract_last(grad_keys, portion[1])
        + contract_last(grad_values, portion[2]),
    )
    grad_norm_one = grad_hidden_one * gain_one.astype(jnp.float32)
    input_grad = grad_after + inv_one * (
        grad_norm_one - norm_one * jnp.mean(grad_norm_one * norm_one, axis=1, keepdims=True)
    )
    gain_term_one = grad_hidden_one * norm_one
    gain_term_two = grad_hidden_two * norm_two
    grad_qkv = jnp.concatenate([grad_queries, grad_keys, grad_values], axis=1)
    grad_gate_up = jnp.concatenate([grad_gate, grad_up], axis=1)
    pick = lambda source_array: source_array
    group_share = lax.psum_scatter(
        jnp.concatenate(
            [
                contract_first(pick(hidden_one), grad_qkv),
                contract_first(pick(grad_attn), mixed),
                contract_first(pick(scaled), grad_gate_up),
                contract_first(pick(cotangent), activated),
                jnp.sum(pick(gain_term_one), axis=0)[:, None],
                jnp.sum(pick(gain_term_two), axis=0)[:, None],
            ],
            axis=1,
        ).astype(jnp.bfloat16),
        "shard",
        scatter_dimension=0,
        tiled=True,
    )
    own_grads = lax.psum(group_share, "rep").astype(jnp.float32)
    edge_two = qk_width + qk_width
    edge_three = edge_two + value_width
    edge_four = edge_three + value_width
    edge_five = edge_four + hidden_width
    edge_six = edge_five + hidden_width
    edge_seven = edge_six + hidden_width
    return (
        block_out,
        input_grad,
        own_grads[:, :qk_width],
        own_grads[:, qk_width:edge_two],
        own_grads[:, edge_two:edge_three],
        own_grads[:, edge_three:edge_four],
        own_grads[:, edge_four:edge_five],
        own_grads[:, edge_five:edge_six],
        own_grads[:, edge_six:edge_seven],
        own_grads[:, edge_seven],
        own_grads[:, edge_seven + 1],
    )


def solution(mesh):
    placed = (
        P(("rep", "shard"), None),
        P("shard", None),
        P("shard", None),
        P("shard", None),
        P("shard", None),
        P("shard", None),
        P("shard", None),
        P("shard", None),
        P("shard"),
        P("shard"),
        P("rep", None),
        P("rep", None),
        P(("rep", "shard"), None),
    )
    return jax.shard_map(
        local,
        mesh=mesh,
        in_specs=placed,
        out_specs=(
            P(("rep", "shard"), None),
            P(("rep", "shard"), None),
            P("shard", None),
            P("shard", None),
            P("shard", None),
            P("shard", None),
            P("shard", None),
            P("shard", None),
            P("shard", None),
            P("shard"),
            P("shard"),
        ),
        check_vma=False,
    )
```

profile of v0, /device:TPU:0, one launch (start us, length us, event | category | flops | bytes accessed | tf_op | source)
XLA Modules:
  0.0 1114.8 jit_solution(6212220869168196635)
XLA Ops:
  10.9 13.5 %all-gather = bf16[8,1,128]{2,1,0:T(2,128)(2,1)S(1)} all-gather(bf16[1,1,128]{2,1,0:T(2,128)(2,1)S(1)} %bitcast.339), channel_id=1, replica_groups=mesh['rep'=4,'shard'=8] {'shard'}, dimensions={0}, use_global_device_ids=true | all-gather | bytes 2304 | tf_op jit(solution)/shard_map/all_gather | solution.py:162
  24.9 17.3 %all_gather.40 = bf16[1024,256]{1,0:T(8,128)(2,1)S(1)} all-gather(bf16[128,256]{1,0:T(8,128)(2,1)S(1)} %copy-done.35), channel_id=1, replica_groups=mesh['rep'=4,'shard'=8] {'shard'}, dimensions={0}, use_global_device_ids=true | all-gather | bytes 589824 | tf_op jit(solution)/shard_map/all_gather | solution.py:160
  74.0 17.6 %all_gather.39 = bf16[1024,256]{1,0:T(8,128)(2,1)S(1)} all-gather(bf16[128,256]{1,0:T(8,128)(2,1)S(1)} %copy-done.36), channel_id=1, replica_groups=mesh['rep'=4,'shard'=8] {'shard'}, dimensions={0}, use_global_device_ids=true | all-gather | bytes 589824 | tf_op jit(solution)/shard_map/all_gather | solution.py:159
  100.2 14.6 %div.136 = bf16[2,512,16,256]{1,0,3,2:T(2,128)(2,1)} reshape(bf16[1024,16,16,16]{0,3,2,1:T(8,128)(2,1)} %multiply_convert_fusion.1) | data formatting | bytes 16777216 | tf_op jit(solution)/shard_map/div | solution.py:29
  114.8 8.6 copy.125
  127.5 9.4 all-gather.2
  140.9 11.8 %pad_maximum_fusion.1 = bf16[2,512,16,273]{1,3,2,0:T(8,128)(2,1)} fusion(bf16[2,512,16,256]{1,3,2,0:T(8,128)(2,1)} %copy.125, bf16[2,512,16,16]{1,3,2,0:T(8,128)(2,1)} %copy.124, bf16[273]{0:T(512)(128)(2,1)S(1)} %pad.12.clone), kind=kLoop, calls=%fused_computation.76 | loop fusion | flops 26836992 | bytes 17859106 | tf_op jit(solution)/shard_map/concatenate | solution.py:25
  156.0 41.7 %while.32 = (s32[]{:T(128)}, f32[4,1024,4,64]{1,3,2,0:T(8,128)}, f32[4,1024,4]{1,2,0:T(4,128)S(1)}, bf16[4,1024,4,64]{1,3,2,0:T(8,128)(2,1)}, bf16[4,1024,4,16]{...) while((s32[]{:T(128)}, f32[4,1024,4,64]{1,3,2,0:T(8,128)}, ...), condition=%wide.region_3.4_spmd.clone, body=%wide.region_1.3_spmd.clone.sunk | while | flops 707784704 | bytes 20764768 | solution.py:202
  235.5 11.5 %fusion.129 = f32[1024,2752]{0,1:T(8,128)} fusion(bf16[1024,2752]{0,1:T(8,128)(2,1)} %all-gather.14.cloned.1.call-done, bf16[1024,1024]{0,1:T(8,128)(2,1)S(1)} %multiply_convert_fusion.6), kind=kOutput, calls=%fused_computation.207 | convolution fusion | flops 5771362304 | bytes 19005440 | tf_op jit(solution)/shard_map/dot_general | solution.py:220
  247.0 26.2 %all-gather.16.cloned.1.call-done = bf16[1024,2752]{0,1:T(8,128)(2,1)} async-done(((bf16[128,2752]{0,1:T(8,128)(2,1)}), bf16[1024,2752]{0,1:T(8,128)(2,1)}) %all-gather.16.cloned.1.call-update) | async-done | bytes 5636112 | tf_op jit(solution)/shard_map/all_gather | solution.py:217
  273.2 11.1 fusion.130
  284.3 48.3 %all-gather.18.cloned.1.call-done = bf16[1024,2752]{0,1:T(8,128)(2,1)} async-done(((bf16[128,2752]{0,1:T(8,128)(2,1)}), bf16[1024,2752]{0,1:T(8,128)(2,1)}) %all-gather.18.cloned.1.call-update) | async-done | bytes 5636112 | tf_op jit(solution)/shard_map/all_gather | solution.py:17
  332.6 20.0 %multiply_convert_fusion.3 = (bf16[1024,2752]{0,1:T(8,128)(2,1)}, bf16[1024,2752]{0,1:T(8,128)(2,1)}, bf16[1024,2752]{0,1:T(8,128)(2,1)}) fusion(f32[1024,2752]{0,1:T(8,128)} %fusion.129, f32[1024,2752]{0,1:T(8,128)} %fusion.130, bf16[1024,1024]{1,0:T(8,128)(2,1)S(1)} %copy-done.25, bf16[1024,2752]{0,1:T(8,128)(2,1)} %all-gather.18.cloned.1.call-done), kind=kOutput, calls=%fused_computation.71 | convolution fusion | flops 5816451072 | bytes 47185920 | tf_op jit(solution)/shard_map/dot_general | solution.py:229
  352.6 11.3 %fusion.128 = f32[1024,1024]{0,1:T(8,128)} fusion(bf16[1024,2752]{0,1:T(8,128)(2,1)} %get-tuple-element.371, bf16[1024,2752]{0,1:T(8,128)(2,1)} %all-gather.14.cloned.1.call-done), kind=kOutput, calls=%fused_computation.206 | convolution fusion | flops 5771362304 | bytes 15466496 | tf_op jit(solution)/shard_map/dot_general | solution.py:36
  363.9 10.8 multiply_reduce_fusion.4
  399.6 152.8 %while.33 = (s32[]{:T(128)}, f32[4,1024,4,16]{1,3,2,0:T(8,128)}, f32[4,1024,4,16]{1,3,2,0:T(8,128)}, f32[4,1024,4,64]{1,3,2,0:T(8,128)}, bf16[4,1024,4,16]{1,3,2...) while((s32[]{:T(128)}, f32[4,1024,4,16]{1,3,2,0:T(8,128)}, ...), condition=%wide.region_8.9_spmd.clone, body=%wide.region_7.8_spmd.clone.sunk | while | flops 1534201856 | bytes 132695256 | solution.py:255
  408.5 10.8 multiply_convert_fusion.10
  446.6 10.8 multiply_convert_fusion.10
  484.7 10.8 multiply_convert_fusion.10
  522.8 10.8 multiply_convert_fusion.10
  569.5 9.2 convolution_convert_fusion.2
  578.7 9.1 copy.164
  594.2 15.3 %copy.165 = f32[2,512,16,273]{1,0,3,2:T(2,128)} copy(f32[2,512,16,273]{1,3,2,0:T(8,128)S(1)} %add_bitcast_fusion.1) | data formatting | bytes 35782656 | tf_op jit(solution)/shard_map/reshape | solution.py:270
  609.5 23.4 %reshape.298 = f32[1024,16,273]{0,2,1:T(8,128)} reshape(f32[2,512,16,273]{1,0,3,2:T(2,128)} %copy.165) | data formatting | bytes 35782656 | tf_op jit(solution)/shard_map/reshape | solution.py:270
  643.0 10.5 fusion.63
  670.2 12.0 %multiply_reduce_fusion.3 = (f32[1024,16,16]{0,2,1:T(8,128)S(1)}, f32[1024,16,16]{0,2,1:T(8,128)S(1)}) fusion(f32[1024,16,16,16]{0,3,2,1:T(8,128)S(1)} %bitcast.295, f32[1024,16,16]{0,2,1:T(8,128)S(1)} %copy-done.8, f32[1024,16,273]{0,2,1:T(8,128)} %reshape.298), kind=kLoop, calls=%fused_computation.64 | loop fusion | flops 20447232 | bytes 37748736 | tf_op jit(solution)/shard_map/transpose(jvp())/reduce_sum | solution.py:23
  682.3 18.4 %convolution_convert_fusion = bf16[1024,5504]{1,0:T(8,128)(2,1)} fusion(bf16[1024,1024]{0,1:T(8,128)(2,1)} %copy-done.27, bf16[1024,2752]{0,1:T(8,128)(2,1)} %get-tuple-element.370, bf16[1024,2752]{0,1:T(8,128)(2,1)} %get-tuple-element.371), kind=kOutput, calls=%fused_computation.67 | convolution fusion | flops 11570905088 | bytes 24641536 | tf_op jit(solution)/shard_map/dot_general | solution.py:42
  720.1 12.1 %multiply_reduce_fusion.1 = (f32[1024,16,16]{0,2,1:T(8,128)S(1)}, f32[1024,16,16]{0,2,1:T(8,128)S(1)}) fusion(f32[1024,16,16,16]{0,3,2,1:T(8,128)} %bitcast.296, f32[1024,16,16]{0,2,1:T(8,128)S(1)} %copy-done.11, f32[1024,16,273]{0,2,1:T(8,128)S(1)} %add_bitcast_fusion), kind=kLoop, calls=%fused_computation.62 | loop fusion | flops 20447232 | bytes 37748736 | tf_op jit(solution)/shard_map/transpose(jvp())/reduce_sum | solution.py:23
  749.1 41.9 %concatenate.35 = bf16[1024,10818]{1,0:T(8,128)(2,1)} concatenate(bf16[1024,1536]{1,0:T(8,128)(2,1)} %convolution_convert_fusion.3, bf16[1024,1024]{1,0:T(8,128)(2,1)} %copy.143, bf16[1024,5504]{1,0:T(8,128)(2,1)} %convolution_convert_fusion, bf16[1024,2752]{1,0:T(8,128)(2,1)} %copy.144, bf16[1024,1]{1,0:T(8,128)(2,1)S(1)} %broadcast_in_dim.128, ...), dimensions={1} | concatenate | bytes 44310528 | tf_op jit(solution)/shard_map/concatenate | solution.py:329
  791.1 218.2 %reduce-scatter.5.cloned.1.call-done = bf16[128,10818]{1,0:T(8,128)(2,1)} async-done(((bf16[1024,10818]{1,0:T(8,128)(2,1)}), bf16[128,10818]{1,0:T(8,128)(2,1)}) %reduce-scatter.5.cloned.1.call-update) | async-done | bytes 2769424 | tf_op jit(solution)/shard_map/reduce_scatter | solution.py:328
  1009.3 11.7 %add_convert_fusion = bf16[1024,1024]{0,1:T(8,128)(2,1)} fusion(f32[1024,1024]{0,1:T(8,128)} %copy-done.12, bf16[1024,2752]{0,1:T(8,128)(2,1)} %get-tuple-element.372, bf16[1024,2752]{0,1:T(8,128)(2,1)} %all-gather.18.cloned.1.call-done), kind=kOutput, calls=%fused_computation.111 | convolution fusion | flops 5773459456 | bytes 17563648 | tf_op jit(solution)/shard_map/dot_general | solution.py:36
  1037.0 55.2 %all-reduce.2.cloned.1.call-done = bf16[128,10818]{1,0:T(8,128)(2,1)} async-done(((bf16[128,10818]{1,0:T(8,128)(2,1)}), bf16[128,10818]{1,0:T(8,128)(2,1)}) %all-reduce.2.cloned.1.call-update) | async-done | bytes 2769424 | tf_op jit(solution)/shard_map/psum | solution.py:344
  (321 shorter events, 383.0 us)
Async XLA Ops:
  7.2 47.4 %all-gather.10.cloned.1.call-start = ((), (), s32[]{:S(2)}) async-start(), calls=%async_computation.2 | async-start | bytes 2359296 | tf_op jit(solution)/shard_map/all_gather | solution.py:161
  7.9 190.4 %all-gather.20.cloned.1.call-start = ((), (), s32[]{:S(2)}) async-start(), calls=%async_computation.10 | async-start | bytes 5806080 | tf_op jit(solution)/shard_map/all_gather | solution.py:183
  10.8 216.3 %copy-start.5 = (bf16[1024,1024]{0,1:T(8,128)(2,1)}, bf16[1024,1024]{0,1:T(8,128)(2,1)S(1)}, u32[]{:S(2)}) copy-start(bf16[1024,1024]{0,1:T(8,128)(2,1)S(1)} %copy.120) | copy-start | bytes 6291460
  24.3 67.3 %copy-start.40 = (f32[8,1,128]{2,1,0:T(1,128)}, f32[8,1,128]{2,1,0:T(1,128)S(1)}, u32[]{:S(2)}) copy-start(f32[8,1,128]{2,1,0:T(1,128)S(1)} %convert_element_type.208) | copy-start | bytes 12292
  24.4 116.6 %copy-start.44 = (bf16[273]{0:T(512)(128)(2,1)}, bf16[273]{0:T(512)(128)(2,1)S(1)}, u32[]{:S(2)}) copy-start(bf16[273]{0:T(512)(128)(2,1)S(1)} %pad.12.clone) | copy-start | bytes 1642
  24.9 66.8 %copy-start.42 = (f32[1024]{0:T(1024)}, f32[1024]{0:T(1024)S(1)}, u32[]{:S(2)}) copy-start(f32[1024]{0:T(1024)S(1)} %add_rsqrt_fusion.1) | copy-start | bytes 12292
  65.7 161.5 %all-gather.12.cloned.1.call-start = ((), (), s32[]{:S(2)}) async-start(), calls=%async_computation.3 | async-start | bytes 2359296 | tf_op jit(solution)/shard_map/all_gather | solution.py:17
  66.4 167.8 %all-gather.14.cloned.1.call-start = ((), (), s32[]{:S(2)}) async-start(), calls=%async_computation.4 | async-start | bytes 6340608 | tf_op jit(solution)/shard_map/all_gather | solution.py:216
  67.0 206.3 %all-gather.16.cloned.1.call-start = ((), (), s32[]{:S(2)}) async-start(), calls=%async_computation.5 | async-start | bytes 6340608 | tf_op jit(solution)/shard_map/all_gather | solution.py:217
  67.6 265.1 %all-gather.18.cloned.1.call-start = ((), (), s32[]{:S(2)}) async-start(), calls=%async_computation.6 | async-start | bytes 6340608 | tf_op jit(solution)/shard_map/all_gather | solution.py:17
  68.1 632.5 %reduce-scatter.3.cloned.1.call-start = ((), (), s32[]{:S(2)}) async-start(), calls=%async_computation.7 | async-start | bytes 7188480 | tf_op jit(solution)/shard_map/reduce_scatter | solution.py:279
  73.3 125.0 %copy-start.51 = (pred[1,8]{1,0:T(4,128)(4,1)}, pred[1,8]{1,0:T(4,128)(4,1)S(1)}, u32[]{:S(2)}) copy-start(pred[1,8]{1,0:T(4,128)(4,1)S(1)} %get-tuple-element.366) | copy-start | bytes 28
  153.4 45.0 %copy-start.47 = (pred[1,8]{1,0:T(4,128)(4,1)}, pred[1,8]{1,0:T(4,128)(4,1)S(1)}, u32[]{:S(2)}) copy-start(pred[1,8]{1,0:T(4,128)(4,1)S(1)} %get-tuple-element.384) | copy-start | bytes 28
  153.4 45.0 %copy-start.49 = (pred[1,8]{1,0:T(4,128)(4,1)}, pred[1,8]{1,0:T(4,128)(4,1)S(1)}, u32[]{:S(2)}) copy-start(pred[1,8]{1,0:T(4,128)(4,1)S(1)} %get-tuple-element.385) | copy-start | bytes 28
  247.0 85.6 %copy-start.25 = (bf16[1024,1024]{1,0:T(8,128)(2,1)S(1)}, bf16[1024,1024]{1,0:T(8,128)(2,1)}, u32[]{:S(2)}) copy-start(bf16[1024,1024]{1,0:T(8,128)(2,1)} %param.29) | copy-start | bytes 6291460
  399.6 152.8 %copy-start.30 = (f32[2,16,1,512]{3,2,1,0:T(1,128)S(1)}, f32[2,16,1,512]{3,2,1,0:T(1,128)}, u32[]{:S(2)}) copy-start(f32[2,16,1,512]{3,2,1,0:T(1,128)} %copy-done.29) | copy-start | bytes 196612
  399.6 152.8 %copy-start.33 = (f32[2,512,16]{1,0,2:T(2,128)S(1)}, f32[2,512,16]{1,0,2:T(2,128)}, u32[]{:S(2)}) copy-start(f32[2,512,16]{1,0,2:T(2,128)} %reshape.269) | copy-start | bytes 196612
  399.6 152.8 %copy-start.34 = (f32[2,512,16]{1,0,2:T(2,128)S(1)}, f32[2,512,16]{1,0,2:T(2,128)}, u32[]{:S(2)}) copy-start(f32[2,512,16]{1,0,2:T(2,128)} %neg.17) | copy-start | bytes 196612
  408.5 23.3 %slice-start = ((s8[16777216]{0:T(1024)(128)(4,1)}), s8[4194304]{0:T(1024)(128)(4,1)S(1)}, s32[]{:S(2)}) async-start(s8[16777216]{0:T(1024)(128)(4,1)} %bitcast.291), calls=%async_computation.11 | async-start | bytes 8388608 | tf_op jit(solution)/shard_map/while
  408.5 23.3 %slice-start.1 = ((s8[16777216]{0:T(1024)(128)(4,1)}), s8[4194304]{0:T(1024)(128)(4,1)S(1)}, s32[]{:S(2)}) async-start(s8[16777216]{0:T(1024)(128)(4,1)} %bitcast.291), calls=%async_computation.12 | async-start | bytes 8388608 | tf_op jit(solution)/shard_map/while
  446.6 23.3 %slice-start = ((s8[16777216]{0:T(1024)(128)(4,1)}), s8[4194304]{0:T(1024)(128)(4,1)S(1)}, s32[]{:S(2)}) async-start(s8[16777216]{0:T(1024)(128)(4,1)} %bitcast.291), calls=%async_computation.11 | async-start | bytes 8388608 | tf_op jit(solution)/shard_map/while
  446.6 23.3 %slice-start.1 = ((s8[16777216]{0:T(1024)(128)(4,1)}), s8[4194304]{0:T(1024)(128)(4,1)S(1)}, s32[]{:S(2)}) async-start(s8[16777216]{0:T(1024)(128)(4,1)} %bitcast.291), calls=%async_computation.12 | async-start | bytes 8388608 | tf_op jit(solution)/shard_map/while
  446.6 23.3 %slice-start.2 = ((s8[16777216]{0:T(1024)(128)(4,1)}), s8[4194304]{0:T(1024)(128)(4,1)S(1)}, s32[]{:S(2)}) async-start(s8[16777216]{0:T(1024)(128)(4,1)} %bitcast.291), calls=%async_computation.13 | async-start | bytes 8388608 | tf_op jit(solution)/shard_map/while
  484.7 23.3 %slice-start = ((s8[16777216]{0:T(1024)(128)(4,1)}), s8[4194304]{0:T(1024)(128)(4,1)S(1)}, s32[]{:S(2)}) async-start(s8[16777216]{0:T(1024)(128)(4,1)} %bitcast.291), calls=%async_computation.11 | async-start | bytes 8388608 | tf_op jit(solution)/shard_map/while
  484.7 23.3 %slice-start.1 = ((s8[16777216]{0:T(1024)(128)(4,1)}), s8[4194304]{0:T(1024)(128)(4,1)S(1)}, s32[]{:S(2)}) async-start(s8[16777216]{0:T(1024)(128)(4,1)} %bitcast.291), calls=%async_computation.12 | async-start | bytes 8388608 | tf_op jit(solution)/shard_map/while
  484.7 23.3 %slice-start.2 = ((s8[16777216]{0:T(1024)(128)(4,1)}), s8[4194304]{0:T(1024)(128)(4,1)S(1)}, s32[]{:S(2)}) async-start(s8[16777216]{0:T(1024)(128)(4,1)} %bitcast.291), calls=%async_computation.13 | async-start | bytes 8388608 | tf_op jit(solution)/shard_map/while
  522.8 23.3 %slice-start = ((s8[16777216]{0:T(1024)(128)(4,1)}), s8[4194304]{0:T(1024)(128)(4,1)S(1)}, s32[]{:S(2)}) async-start(s8[16777216]{0:T(1024)(128)(4,1)} %bitcast.291), calls=%async_computation.11 | async-start | bytes 8388608 | tf_op jit(solution)/shard_map/while
  522.8 23.3 %slice-start.1 = ((s8[16777216]{0:T(1024)(128)(4,1)}), s8[4194304]{0:T(1024)(128)(4,1)S(1)}, s32[]{:S(2)}) async-start(s8[16777216]{0:T(1024)(128)(4,1)} %bitcast.291), calls=%async_computation.12 | async-start | bytes 8388608 | tf_op jit(solution)/shard_map/while
  522.8 23.3 %slice-start.2 = ((s8[16777216]{0:T(1024)(128)(4,1)}), s8[4194304]{0:T(1024)(128)(4,1)S(1)}, s32[]{:S(2)}) async-start(s8[16777216]{0:T(1024)(128)(4,1)} %bitcast.291), calls=%async_computation.13 | async-start | bytes 8388608 | tf_op jit(solution)/shard_map/while
  587.8 421.5 %reduce-scatter.5.cloned.1.call-start = ((), (), s32[]{:S(2)}) async-start(), calls=%async_computation.8 | async-start | bytes 25067520 | tf_op jit(solution)/shard_map/reduce_scatter | solution.py:328
  609.5 23.4 %copy-start.22 = (bf16[1024,1024]{0,1:T(8,128)(2,1)S(1)}, bf16[1024,1024]{0,1:T(8,128)(2,1)}, u32[]{:S(2)}) copy-start(bf16[1024,1024]{0,1:T(8,128)(2,1)} %fusion.75) | copy-start | bytes 6291460
  791.0 301.1 %all-reduce.2.cloned.1.call-start = ((), (), s32[]{:S(2)}) async-start(), calls=%async_computation.9 | async-start | bytes 5570560 | tf_op jit(solution)/shard_map/psum | solution.py:344
  (56 other events, 379.5 us)
Sparse Core Ops, SparseCore 0:
  9.6 36.0 all-gather.9
  65.8 57.8 all-gather.19
  125.3 27.8 all-gather.11
  154.7 59.1 all-gather.13
  215.3 57.9 all-gather.15
  274.7 57.9 all-gather.17
  588.0 69.0 reduce-scatter.2
  791.2 218.1 reduce-scatter.4
  1012.5 79.6 all-reduce.1
where the time goes:
time: 1130 us; the launch traced here: 1110 us
  matrix products  391 us (35%)
  waiting for transfers between devices  351 us (31%)
  local copies, waits for them, and re-layouts  204 us (18%)
  other arithmetic  90.3 us (8%)
  blocking collectives  57.8 us (5%)
  between operations  19.1 us (2%)
    reduce_scatter x1, waiting for transfers between devices, local(): lax.psum_scatter(jnp.concatenate([contract_first(pick(hidden_one), grad_q...  218 us
    dot_general x8, matrix products, kernel_of(): jnp.einsum('thf,uhf->htu', queries, key_heads, preferred_element_type=jnp...  57.4 us
    psum x1, waiting for transfers between devices, local(): own_grads = lax.psum(group_share, 'rep').astype(jnp.float32)  55.2 us
    all_gather x2, waiting for transfers between devices, on_whole(): whole = lax.all_gather(value, axis, axis=dim, tiled=True)  48.3 us
    dot_general x7, matrix products, contract_last(): lax.dot_general(left, right, (((1,), (1,)), ((), ())), preferred_element_...  44.6 us
    dot_general x4, matrix products, local_backward(): jnp.einsum('the,uhe->htu', grad_num, value_heads, preferred_element_type=...  43.1 us
    concatenate x1, local copies, waits for them, and re-layouts, local(): jnp.concatenate([contract_first(pick(hidden_one), grad_qkv), contract_fir...  41.9 us
    dot_general x4, matrix products, contract_first(): lax.dot_general(left, right, (((0,), (0,)), ((), ())), preferred_element_...  40.9 us
  transfers between devices with their start and end apart: 9, of which 4 were waited for; matrix products, arithmetic and copies ran while one was open for 28% of the time, Pallas kernels for 0%

commit v1 on v0

v1 whole, which is shorter than its diff:
```python
from functools import partial
import math

import jax
import jax.numpy as jnp
import numpy as np
from jax import lax
from jax.experimental import pallas as pl
from jax.experimental.pallas import tpu as pltpu
from jax.sharding import PartitionSpec as P

HEADS = 16
FEAT = 16
CONT_PER = 4
CHUNK = 256
FPAD = 256
FROWS = 160

norm_eps = 1e-05

f32 = jnp.float32
bf16 = jnp.bfloat16


def feature_table():
    table = np.zeros((8, FPAD), np.float32)
    table[0:2] = -1000.0
    table[2, 0] = table[3, 0] = table[4, 0] = table[5, 0] = 1.0
    at = 1
    for a in range(FEAT):
        table[0, at] = a
        table[3, at] = 1.0
        table[4, at] = table[5, at] = 0.5
        at += 1
    for a in range(FEAT):
        for b in range(a, FEAT):
            table[0, at] = a
            table[1, at] = b
            table[4, at] = 1.0 / (4.0 * math.sqrt(2.0))
            table[5, at] = table[4, at] * (1.0 if a == b else 2.0)
            at += 1
    return table


def mm(left, right):
    return lax.dot_general(left, right, (((1,), (0,)), ((), ())), preferred_element_type=f32)


def mm_nt(left, right):
    return lax.dot_general(left, right, (((1,), (1,)), ((), ())), preferred_element_type=f32)


def mm_tn(left, right):
    return lax.dot_general(left, right, (((0,), (0,)), ((), ())), preferred_element_type=f32)


def pick_rows(index_row, head, width):
    rows = lax.broadcasted_iota(jnp.int32, (width, FPAD), 0)
    return jnp.where(rows == index_row.astype(jnp.int32) + FEAT * head, 1.0, 0.0).astype(bf16)


def pick_cols(index_col, head, width):
    cols = lax.broadcasted_iota(jnp.int32, (FPAD, width), 1)
    return jnp.where(cols == index_col.astype(jnp.int32) + FEAT * head, 1.0, 0.0).astype(bf16)


def half_lanes(shape, half):
    lanes = lax.broadcasted_iota(jnp.int32, shape, len(shape) - 1)
    return ((lanes // 64) % 2) == half


def pair_join(first, second):
    return jnp.where(half_lanes(first.shape, 0), first, second)


def feats_t(tab, source_t, head):
    width = source_t.shape[0]
    first = mm(pick_cols(tab[:, 0:1], head, width), source_t) + tab[:, 2:3]
    second = mm(pick_cols(tab[:, 1:2], head, width), source_t) + tab[:, 3:4]
    return first * second


def state_kernel(flag_ref, tab_ref, kt_ref, v_ref, tot_ref, totz_ref, pre_ref, prez_ref):
    pair = pl.program_id(0)
    prompt = flag_ref[0].astype(f32)
    tab = tab_ref[...]
    chunks = v_ref.shape[0] // CHUNK
    sums = []
    feats = []
    for h in range(2):
        feats.append((feats_t(tab, kt_ref[...], 2 * pair + h) * tab[:, 4:5]).astype(bf16))
    for j in range(chunks):
        rows = slice(j * CHUNK, (j + 1) * CHUNK)
        values = v_ref[rows, :]
        ext = jnp.concatenate([values, jnp.ones_like(values)], axis=1)
        sums.append(pair_join(mm(feats[0][:, rows], ext), mm(feats[1][:, rows], ext)))
    first = sums[0] + sums[1]
    second = sums[2] + sums[3]
    total = first + second
    tot_ref[...] = total[:FROWS, :128].astype(bf16)
    lanes = lax.broadcasted_iota(jnp.int32, (FROWS, 128), 1)
    norms = total[:FROWS, 128:]
    shifted = jnp.where(
        lanes == 2 * pair,
        jnp.broadcast_to(norms[:, 0:1], norms.shape),
        jnp.where(lanes == 2 * pair + 1, jnp.broadcast_to(norms[:, 64:65], norms.shape), 0.0),
    ).astype(bf16)

    @pl.when(pair == 0)
    def _():
        totz_ref[...] = shifted

    @pl.when(pair > 0)
    def _():
        totz_ref[...] = totz_ref[...] + shifted

    prefix = [sums[0], first * prompt, first * prompt + sums[2]]
    for i in range(3):
        pre_ref[i] = prefix[i][:FROWS, :128].astype(bf16)
        prez_ref[i] = prefix[i][:FROWS, 128:].astype(bf16)


def running_states(pair, prompt, sin_ref, sinz_ref, pre_ref, prez_ref):
    lanes = lax.broadcasted_iota(jnp.int32, (128, 128), 0)
    wanted = 2 * pair + lax.broadcasted_iota(jnp.int32, (128, 128), 1) // 64
    spread = jnp.where(lanes == wanted, 1.0, 0.0).astype(bf16)
    base = []
    for n in range(2):
        norms = mm(sinz_ref[n], spread)
        base.append(jnp.concatenate([sin_ref[n].astype(f32), norms], axis=1))
    pad = jnp.zeros((FPAD - FROWS, 256), bf16)
    states = []
    for i in range(4):
        state = base[i // 2]
        if i >= 2:
            state = jnp.where(prompt > 0.5, base[0], base[1])
        if i >= 1:
            state = state + jnp.concatenate([pre_ref[i - 1], prez_ref[i - 1]], axis=1).astype(f32)
        states.append(jnp.concatenate([state.astype(bf16), pad], axis=0))
    return states


def head_lanes(head, shape):
    return (lax.broadcasted_iota(jnp.int32, shape, 1) // FEAT) == head


def causal(shape):
    return lax.broadcasted_iota(jnp.int32, shape, 1) <= lax.broadcasted_iota(jnp.int32, shape, 0)


def forward_kernel(
    flag_ref, tabr_ref, q_ref, kt_ref, v_ref, sin_ref, sinz_ref, pre_ref, prez_ref, y_ref, rden_ref
):
    pair = pl.program_id(0)
    prompt = flag_ref[0].astype(f32)
    tab = tabr_ref[...]
    states = running_states(pair, prompt, sin_ref, sinz_ref, pre_ref, prez_ref)
    width = q_ref.shape[1]
    allowed = causal((CHUNK, CHUNK))
    picks = [
        (pick_rows(tab[0:1], 2 * pair + h, width), pick_rows(tab[1:2], 2 * pair + h, width))
        for h in range(2)
    ]
    for i in range(4):
        rows = slice(i * CHUNK, (i + 1) * CHUNK)
        queries = q_ref[rows, :]
        values = v_ref[rows, :]
        ext = jnp.concatenate([values, jnp.ones_like(values)], axis=1)
        sums = []
        for h in range(2):
            head = 2 * pair + h
            masked = jnp.where(head_lanes(head, queries.shape), queries.astype(f32) * 0.25, 0.0)
            one_plus = mm(masked.astype(bf16), kt_ref[:, rows]) + 1.0
            kernel = jnp.where(allowed, 0.5 * one_plus * one_plus + 0.5, 0.0).astype(bf16)
            first = mm(queries, picks[h][0]) + tab[2:3]
            second = mm(queries, picks[h][1]) + tab[3:4]
            feats = (first * second * tab[5:6]).astype(bf16)
            sums.append(mm(kernel, ext) + mm(feats, states[i]))
        both = pair_join(sums[0], sums[1])
        rden = 1.0 / both[:, 128:]
        y_ref[rows, :] = (both[:, :128] * rden).astype(bf16)
        rden_ref[rows, :] = rden


def grad_state_kernel(
    flag_ref, tab_ref, qt_ref, dy_ref, y_ref, rden_ref,
    dnum_ref, dden_ref, tot_ref, totz_ref, suf_ref, sufz_ref,
):
    pair = pl.program_id(0)
    prompt = flag_ref[0].astype(f32)
    tab = tab_ref[...]
    rden = rden_ref[...]
    dy = dy_ref[...]
    prod = dy * y_ref[...].astype(f32)
    high = prod.astype(bf16)
    low = (prod - high.astype(f32)).astype(bf16)
    rows_half = (lax.broadcasted_iota(jnp.int32, (256, 128), 0) // 64) % 2
    lanes_half = lax.broadcasted_iota(jnp.int32, (256, 128), 1) // 64
    ones = jnp.where(rows_half == lanes_half, 1.0, 0.0).astype(bf16)
    total = mm(jnp.concatenate([high, low], axis=1), ones)
    dden = (-total * rden).astype(bf16)
    dnum = (dy * rden).astype(bf16)
    dnum_ref[...] = dnum
    dden_ref[...] = dden
    feats = []
    for h in range(2):
        feats.append((feats_t(tab, qt_ref[...], 2 * pair + h) * tab[:, 5:6]).astype(bf16))
    ext = jnp.concatenate([dnum, dden], axis=1)
    sums = []
    for i in range(4):
        rows = slice(i * CHUNK, (i + 1) * CHUNK)
        sums.append(pair_join(mm(feats[0][:, rows], ext[rows]), mm(feats[1][:, rows], ext[rows])))
    first = sums[0] + sums[1]
    second = sums[2] + sums[3]
    totals = [first + second * prompt, second * (1.0 - prompt)]
    lanes = lax.broadcasted_iota(jnp.int32, (FROWS, 128), 1)
    for n in range(2):
        tot_ref[n] = totals[n][:FROWS, :128].astype(bf16)
        norms = totals[n][:FROWS, 128:]
        shifted = jnp.where(
            lanes == 2 * pair,
            jnp.broadcast_to(norms[:, 0:1], norms.shape),
            jnp.where(lanes == 2 * pair + 1, jnp.broadcast_to(norms[:, 64:65], norms.shape), 0.0),
        ).astype(bf16)

        @pl.when(pair == 0)
        def _():
            totz_ref[n] = shifted

        @pl.when(pair > 0)
        def _():
            totz_ref[n] = totz_ref[n] + shifted

    suffix = [sums[1] + second * prompt, second * prompt, sums[3]]
    for i in range(3):
        suf_ref[i] = suffix[i][:FROWS, :128].astype(bf16)
        sufz_ref[i] = suffix[i][:FROWS, 128:].astype(bf16)


def backward_kernel(
    flag_ref, tab_ref, tabr_ref, q_ref, k_ref, kt_ref, v_ref, dnum_ref, dden_ref,
    sin_ref, sinz_ref, pre_ref, prez_ref, dp_ref, dpz_ref, suf_ref, sufz_ref,
    dq_ref, dk_ref, dv_ref, dq_acc, dk_acc,
):
    pair = pl.program_id(0)
    prompt = flag_ref[0].astype(f32)
    tabr = tabr_ref[...]
    tab = tab_ref[...]
    width = q_ref.shape[1]
    states = running_states(pair, prompt, sin_ref, sinz_ref, pre_ref, prez_ref)

    lanes = lax.broadcasted_iota(jnp.int32, (128, 128), 0)
    wanted = 2 * pair + lax.broadcasted_iota(jnp.int32, (128, 128), 1) // 64
    spread = jnp.where(lanes == wanted, 1.0, 0.0).astype(bf16)
    from_readers = jnp.concatenate([dp_ref[...].astype(f32), mm(dpz_ref[...], spread)], axis=1)
    pad = jnp.zeros((FPAD - FROWS, 256), bf16)
    grad_states = []
    for i in range(4):
        state = from_readers
        if i < 3:
            state = state + jnp.concatenate([suf_ref[i], sufz_ref[i]], axis=1).astype(f32)
        grad_states.append(jnp.concatenate([state.astype(bf16), pad], axis=0))

    allowed = causal((CHUNK, CHUNK))
    wide = lax.broadcasted_iota(jnp.int32, (CHUNK, 256), 1)

    @pl.when(pair == 0)
    def _():
        dq_acc[...] = jnp.zeros_like(dq_acc)
        dk_acc[...] = jnp.zeros_like(dk_acc)

    picks = []
    for h in range(2):
        head = 2 * pair + h
        picks.append(
            (
                pick_rows(tabr[0:1], head, width),
                pick_rows(tabr[1:2], head, width),
                pick_cols(tab[:, 0:1], head, width),
                pick_cols(tab[:, 1:2], head, width),
            )
        )
    for i in range(4):
        rows = slice(i * CHUNK, (i + 1) * CHUNK)
        queries = q_ref[rows, :]
        keys = k_ref[rows, :]
        values = v_ref[rows, :]
        ext = jnp.concatenate([values, jnp.ones_like(values)], axis=1)
        grads = jnp.concatenate([dnum_ref[rows, :], dden_ref[rows, :]], axis=1)
        dvs = []
        dq = None
        dk = None
        for h in range(2):
            head = 2 * pair + h
            mine = (wide // 64 == h) | (wide == 128 + 64 * h)
            in_head = head_lanes(head, queries.shape)
            q_head = jnp.where(in_head, queries.astype(f32) * 0.25, 0.0).astype(bf16)
            k_head = jnp.where(in_head, keys.astype(f32) * 0.25, 0.0).astype(bf16)
            grads_head = jnp.where(mine, grads, jnp.zeros_like(grads))
            ext_head = jnp.where(mine, ext, jnp.zeros_like(ext))
            one_plus = mm(q_head, kt_ref[:, rows]) + 1.0
            kernel = jnp.where(allowed, 0.5 * one_plus * one_plus + 0.5, 0.0).astype(bf16)
            dscore = jnp.where(allowed, mm_nt(grads_head, ext) * one_plus, 0.0).astype(bf16)
            pick_a, pick_b, back_a, back_b = picks[h]
            qa = mm(queries, pick_a) + tabr[2:3]
            qb = mm(queries, pick_b) + tabr[3:4]
            dfq = mm_nt(grads_head, states[i]) * tabr[5:6]
            ka = mm(keys, pick_a) + tabr[2:3]
            kb = mm(keys, pick_b) + tabr[3:4]
            fk = (ka * kb * tabr[4:5]).astype(bf16)
            dfk = mm_nt(ext_head, grad_states[i]) * tabr[4:5]
            dq_h = (
                mm(dscore, k_head)
                + mm((dfq * qb).astype(bf16), back_a)
                + mm((dfq * qa).astype(bf16), back_b)
            )
            dk_h = (
                mm_tn(dscore, q_head)
                + mm((dfk * kb).astype(bf16), back_a)
                + mm((dfk * ka).astype(bf16), back_b)
            )
            dq = dq_h if dq is None else dq + dq_h
            dk = dk_h if dk is None else dk + dk_h
            dvs.append(mm_tn(kernel, grads[:, :128]) + mm(fk, grad_states[i][:, :128]))
        dq_acc[rows, :] += dq
        dk_acc[rows, :] += dk
        dv_ref[rows, :] = pair_join(dvs[0], dvs[1]).astype(bf16)

    @pl.when(pair == pl.num_programs(0) - 1)
    def _():
        dq_ref[...] = dq_acc[...].astype(bf16)
        dk_ref[...] = dk_acc[...].astype(bf16)


def smem_spec():
    return pl.BlockSpec(memory_space=pltpu.SMEM)


def full_spec(shape):
    return pl.BlockSpec(shape, lambda p: (0,) * len(shape))


def lane_spec(shape):
    return pl.BlockSpec(shape, lambda p: (0,) * (len(shape) - 1) + (p,))


def shaped(shape, dtype):
    return jax.ShapeDtypeStruct(shape, dtype)


def cost(flops, moved):
    return pl.CostEstimate(flops=flops, bytes_accessed=moved, transcendentals=0)


PAIR_PASS = 2 * 256 * 256 * 256 * 4 * HEADS


def make_states(flag, table_t, keys_t, values):
    tok, width = values.shape
    pairs = width // 128
    return pl.pallas_call(
        state_kernel,
        grid=(pairs,),
        in_specs=[
            smem_spec(),
            full_spec((FPAD, 8)),
            full_spec(keys_t.shape),
            lane_spec((tok, 128)),
        ],
        out_specs=[
            lane_spec((FROWS, 128)),
            full_spec((FROWS, 128)),
            lane_spec((3, FROWS, 128)),
            lane_spec((3, FROWS, 128)),
        ],
        out_shape=[
            shaped((FROWS, width), bf16),
            shaped((FROWS, 128), bf16),
            shaped((3, FROWS, width), bf16),
            shaped((3, FROWS, width), bf16),
        ],
        cost_estimate=cost(3 * PAIR_PASS, 6 << 20),
        name="piece_states",
    )(flag, table_t, keys_t, values)


def attend(flag, table, queries, keys_t, values, states, norms, prefix, prefix_z):
    tok, width = values.shape
    return pl.pallas_call(
        forward_kernel,
        grid=(width // 128,),
        in_specs=[
            smem_spec(),
            full_spec((8, FPAD)),
            full_spec(queries.shape),
            full_spec(keys_t.shape),
            lane_spec((tok, 128)),
            lane_spec((2, FROWS, 128)),
            full_spec((2, FROWS, 128)),
            lane_spec((3, FROWS, 128)),
            lane_spec((3, FROWS, 128)),
        ],
        out_specs=[lane_spec((tok, 128)), lane_spec((tok, 128))],
        out_shape=[shaped((tok, width), bf16), shaped((tok, width), f32)],
        cost_estimate=cost(5 * PAIR_PASS, 14 << 20),
        name="attend_forward",
    )(flag, table, queries, keys_t, values, states, norms, prefix, prefix_z)


def grad_states_of(flag, table_t, queries_t, dy, mixed, rden):
    tok, width = mixed.shape
    return pl.pallas_call(
        grad_state_kernel,
        grid=(width // 128,),
        in_specs=[
            smem_spec(),
            full_spec((FPAD, 8)),
            full_spec(queries_t.shape),
            lane_spec((tok, 128)),
            lane_spec((tok, 128)),
            lane_spec((tok, 128)),
        ],
        out_specs=[
            lane_spec((tok, 128)),
            lane_spec((tok, 128)),
            lane_spec((2, FROWS, 128)),
            full_spec((2, FROWS, 128)),
            lane_spec((3, FROWS, 128)),
            lane_spec((3, FROWS, 128)),
        ],
        out_shape=[
            shaped((tok, width), bf16),
            shaped((tok, width), bf16),
            shaped((2, FROWS, width), bf16),
            shaped((2, FROWS, 128), bf16),
            shaped((3, FROWS, width), bf16),
            shaped((3, FROWS, width), bf16),
        ],
        cost_estimate=cost(3 * PAIR_PASS, 18 << 20),
        name="state_gradients",
    )(flag, table_t, queries_t, dy, mixed, rden)


def attend_backward(
    flag, table_t, table, queries, keys, keys_t, values, dnum, dden,
    states, norms, prefix, prefix_z, dp, dpz, suffix, suffix_z,
):
    tok, width = values.shape
    qk = queries.shape[1]
    return pl.pallas_call(
        backward_kernel,
        grid=(width // 128,),
        in_specs=[
            smem_spec(),
            full_spec((FPAD, 8)),
            full_spec((8, FPAD)),
            full_spec(queries.shape),
            full_spec(keys.shape),
            full_spec(keys_t.shape),
            lane_spec((tok, 128)),
            lane_spec((tok, 128)),
            lane_spec((tok, 128)),
            lane_spec((2, FROWS, 128)),
            full_spec((2, FROWS, 128)),
            lane_spec((3, FROWS, 128)),
            lane_spec((3, FROWS, 128)),
            lane_spec((FROWS, 128)),
            full_spec((FROWS, 128)),
            lane_spec((3, FROWS, 128)),
            lane_spec((3, FROWS, 128)),
        ],
        out_specs=[full_spec((tok, qk)), full_spec((tok, qk)), lane_spec((tok, 128))],
        out_shape=[
            shaped((tok, qk), bf16),
            shaped((tok, qk), bf16),
            shaped((tok, width), bf16),
        ],
        scratch_shapes=[pltpu.VMEM((tok, qk), f32), pltpu.VMEM((tok, qk), f32)],
        cost_estimate=cost(16 * PAIR_PASS, 16 << 20),
        name="attend_backward",
    )(
        flag, table_t, table, queries, keys, keys_t, values, dnum, dden,
        states, norms, prefix, prefix_z, dp, dpz, suffix, suffix_z,
    )


def gather_rows(part):
    return lax.all_gather(part, "shard", axis=0, tiled=True)


def reduce_rows(grad):
    share = lax.psum_scatter(grad.astype(bf16), "shard", scatter_dimension=0, tiled=True)
    return lax.psum(share, "rep").astype(f32)


def local(
    inputs,
    query_weight,
    key_weight,
    value_weight,
    out_weight,
    gate_weight,
    up_weight,
    down_weight,
    attn_gain,
    mlp_gain,
    slot_of,
    parent_of,
    cotangent,
):
    tok_rows, width = inputs.shape
    qk_width = query_weight.shape[1]
    value_width = value_weight.shape[1]
    shards = lax.axis_size("shard")
    own_index = lax.axis_index("shard")
    slot_ids = slot_of[0]
    parent_ids = parent_of[0]
    prompt_slots = shards // 2
    pieces_per = CONT_PER // 2
    own_slot = lax.dynamic_index_in_dim(slot_ids, own_index, keepdims=False)
    own_prompt = own_slot < prompt_slots
    source_prompt = slot_ids < prompt_slots
    source_family = slot_ids // pieces_per
    earlier = (
        source_prompt
        & (source_family == own_slot // pieces_per)
        & (slot_ids % pieces_per < own_slot % pieces_per)
    )
    pair_index = jnp.clip(own_slot - prompt_slots, 0, shards // 2 - 1)
    first_parent = lax.dynamic_index_in_dim(parent_ids, 2 * pair_index, keepdims=False)
    second_parent = lax.dynamic_index_in_dim(parent_ids, 2 * pair_index + 1, keepdims=False)
    from_first = source_prompt & (source_family == first_parent)
    from_second = source_prompt & (source_family == second_parent)
    source_mix = jnp.where(
        own_prompt, jnp.stack([earlier, earlier]), jnp.stack([from_first, from_second])
    ).astype(f32)
    flag = own_prompt.astype(jnp.int32).reshape(1)
    table_np = feature_table()
    table = jnp.asarray(table_np)
    table_t = jnp.asarray(np.ascontiguousarray(table_np.T))

    gains = jnp.zeros((attn_gain.shape[0], 128), bf16)
    gains = gains.at[:, 0].set(attn_gain).at[:, 1].set(mlp_gain)
    packed = gather_rows(jnp.concatenate([query_weight, key_weight, value_weight, gains], axis=1))
    qkv_width = 2 * qk_width + value_width
    qkv_weight = packed[:, :qkv_width]
    gain_one = packed[:, qkv_width].astype(f32)[None]
    gain_two = packed[:, qkv_width + 1].astype(f32)[None]
    out_full = gather_rows(out_weight)
    down_full = gather_rows(down_weight)
    gate_full = gather_rows(gate_weight)
    up_full = gather_rows(up_weight)

    x = inputs.astype(f32)
    inv_one = lax.rsqrt(jnp.mean(x * x, axis=1, keepdims=True) + norm_eps)
    norm_one = x * inv_one
    hidden_one = (norm_one * gain_one).astype(bf16)
    qkv = mm(hidden_one, qkv_weight).astype(bf16)
    queries = qkv[:, :qk_width]
    keys = qkv[:, qk_width : 2 * qk_width]
    values = qkv[:, 2 * qk_width :]
    queries_t = queries.T
    keys_t = keys.T

    total, total_z, prefix, prefix_z = make_states(flag, table_t, keys_t, values)
    own_state = jnp.concatenate([total, total_z], axis=1)
    all_states = lax.all_gather(own_state, "shard", axis=0, tiled=False)
    used = jnp.einsum(
        "sn,nfl->sfl", source_mix.astype(bf16), all_states, preferred_element_type=f32
    ).astype(bf16)
    used_states = used[:, :, :value_width]
    used_norms = used[:, :, value_width:]
    mixed, rden = attend(
        flag, table, queries, keys_t, values, used_states, used_norms, prefix, prefix_z
    )

    after_attn = x + mm_nt(mixed, out_full)
    inv_two = lax.rsqrt(jnp.mean(after_attn * after_attn, axis=1, keepdims=True) + norm_eps)
    norm_two = after_attn * inv_two
    hidden_two = (norm_two * gain_two).astype(bf16)
    gate_pre = mm(hidden_two, gate_full)
    up_pre = mm(hidden_two, up_full)
    sigma = jax.nn.sigmoid(gate_pre)
    activated = (gate_pre * sigma * up_pre).astype(bf16)
    grad_act = mm(cotangent, down_full)
    down_grad = reduce_rows(mm_tn(cotangent, activated))
    grad_up = (grad_act * gate_pre * sigma).astype(bf16)
    grad_gate = (grad_act * up_pre * sigma * (1.0 + gate_pre * (1.0 - sigma))).astype(bf16)
    up_grad = reduce_rows(mm_tn(hidden_two, grad_up))
    gate_grad = reduce_rows(mm_tn(hidden_two, grad_gate))
    block_out = (after_attn + mm_nt(activated, down_full)).astype(bf16)

    grad_hidden_two = mm_nt(grad_gate, gate_full) + mm_nt(grad_up, up_full)
    grad_norm_two = grad_hidden_two * gain_two
    grad_after = cotangent.astype(f32) + inv_two * (
        grad_norm_two - norm_two * jnp.mean(grad_norm_two * norm_two, axis=1, keepdims=True)
    )
    grad_attn = grad_after.astype(bf16)
    out_grad = reduce_rows(mm_tn(grad_attn, mixed))
    dy = mm(grad_attn, out_full)
    dnum, dden, dstate, dstate_z, suffix, suffix_z = grad_states_of(
        flag, table_t, queries_t, dy, mixed, rden
    )
    grad_slots = jnp.concatenate([dstate, dstate_z], axis=2)
    to_sources = jnp.einsum(
        "sn,sfl->nfl", source_mix.astype(bf16), grad_slots, preferred_element_type=f32
    ).astype(bf16)
    grad_piece = lax.psum_scatter(to_sources, "shard", scatter_dimension=0, tiled=False)
    dq, dk, dv = attend_backward(
        flag, table_t, table, queries, keys, keys_t, values, dnum, dden,
        used_states, used_norms, prefix, prefix_z,
        grad_piece[:, :value_width], grad_piece[:, value_width:], suffix, suffix_z,
    )
    grad_qkv = jnp.concatenate([dq, dk, dv], axis=1)
    grad_hidden_one = mm_nt(grad_qkv, qkv_weight)
    grad_norm_one = grad_hidden_one * gain_one
    input_grad = grad_after + inv_one * (
        grad_norm_one - norm_one * jnp.mean(grad_norm_one * norm_one, axis=1, keepdims=True)
    )
    gain_grads = jnp.stack(
        [
            jnp.sum(grad_hidden_one * norm_one, axis=0),
            jnp.sum(grad_hidden_two * norm_two, axis=0),
        ],
        axis=1,
    )
    last = reduce_rows(
        jnp.concatenate(
            [
                mm_tn(hidden_one, grad_qkv).astype(bf16),
                jnp.pad(gain_grads, ((0, 0), (0, 126))).astype(bf16),
            ],
            axis=1,
        )
    )
    return (
        block_out,
        input_grad,
        last[:, :qk_width],
        last[:, qk_width : 2 * qk_width],
        last[:, 2 * qk_width : qkv_width],
        out_grad,
        gate_grad,
        up_grad,
        down_grad,
        last[:, qkv_width],
        last[:, qkv_width + 1],
    )


def solution(mesh):
    placed = (P(("rep", "shard"), None),) + (P("shard", None),) * 7 + (P("shard"),) * 2
    placed = placed + (P("rep", None),) * 2 + (P(("rep", "shard"), None),)
    return jax.shard_map(
        local,
        mesh=mesh,
        in_specs=placed,
        out_specs=(P(("rep", "shard"), None),) * 2
        + (P("shard", None),) * 7
        + (P("shard"),) * 2,
        check_vma=False,
    )
```

time: 1130 us -> 815 us (0.72)
  matrix products: 391 us -> 141 us
  local copies, waits for them, and re-layouts: 204 us -> 75 us
  waiting for transfers between devices: 351 us -> 449 us
  Pallas kernels: 0 us -> 95.5 us
  other arithmetic: 90.3 us -> 28.4 us
  blocking collectives: 57.8 us -> 0 us
    dot_general x57 -> x17, matrix products: 391 us -> 141 us  [the longest x5 53 us: mm(): lax.dot_general(left, right, (((1,), (0,)), ((), ())), preferred_element_...]
    reduce_scatter x2 -> x3, waiting for transfers between devices: 218 us -> 77.8 us  [the longest x2 77.8 us: reduce_rows(): lax.psum_scatter(grad.astype(bf16), 'shard', scatter_dimension=0, tiled=T...]
    all_gather x6, waiting for transfers between devices: 74.6 us -> 213 us  [the longest x5 191 us: gather_rows(): return lax.all_gather(part, 'shard', axis=0, tiled=True)]
    unnamed x9 -> x16, waiting for transfers between devices: 3.01 us -> 101 us
    pallas_call x0 -> x4, Pallas kernels: none -> 95.5 us  [the longest x1 47 us: attend_backward(): pl.pallas_call(backward_kernel, grid=(width // 128,), in_specs=[smem_spec...]
    all_gather x4 -> x0, blocking collectives: 57.8 us -> none  [the longest x1 17.6 us: local(): part_query = lax.all_gather(query_weight, 'shard', axis=0, tiled=True)]
    reshape x9 -> x0, local copies, waits for them, and re-layouts: 50.8 us -> none  [the longest x2 38.7 us: local(): grad_query_feat = (jnp.einsum('nthe,nhef->nthf', halves_num, used_values,...]
    concatenate x2 -> x1, local copies, waits for them, and re-layouts: 41.9 us -> 1.81 us  [local(): grad_qkv = jnp.concatenate([dq, dk, dv], axis=1)]
  transfers between devices with their start and end apart: 9 -> 13, of which waited for: 4 -> 11; matrix products, arithmetic and copies ran while one was open for 28% -> 20% of each run, Pallas kernels for 0% -> 8%
where the time goes in v1:
time: 815 us; the launch traced here: 809 us
  waiting for transfers between devices  449 us (55%)
  matrix products  141 us (17%)
  Pallas kernels  95.5 us (12%)
  local copies, waits for them, and re-layouts  75 us (9%)
  other arithmetic  28.4 us (3%)
  between operations  18.7 us (2%)
    all_gather x5, waiting for transfers between devices, gather_rows(): return lax.all_gather(part, 'shard', axis=0, tiled=True)  191 us
    unnamed x16, waiting for transfers between devices  101 us
    reduce_scatter x2, waiting for transfers between devices, reduce_rows(): lax.psum_scatter(grad.astype(bf16), 'shard', scatter_dimension=0, tiled=T...  77.8 us
    psum x1, waiting for transfers between devices, reduce_rows(): return lax.psum(share, 'rep').astype(f32)  57.5 us
    unnamed x58, local copies, waits for them, and re-layouts  57.1 us
    dot_general x5, matrix products, mm(): lax.dot_general(left, right, (((1,), (0,)), ((), ())), preferred_element_...  53 us
    pallas_call x1, Pallas kernels, attend_backward(): pl.pallas_call(backward_kernel, grid=(width // 128,), in_specs=[smem_spec...  47 us
    dot_general x5, matrix products, mm_tn(): lax.dot_general(left, right, (((0,), (0,)), ((), ())), preferred_element_...  42.9 us
  transfers between devices with their start and end apart: 13, of which 11 were waited for; matrix products, arithmetic and copies ran while one was open for 20% of the time, Pallas kernels for 8%

profile of v1, /device:TPU:0, one launch (start us, length us, event | category | flops | bytes accessed | tf_op | source)
XLA Modules:
  0.0 808.8 jit_solution(2010490542405932914)
XLA Ops:
  17.9 38.5 %all-gather.8.cloned.1.call-done = bf16[1024,1664]{1,0:T(8,128)(2,1)} async-done(((bf16[128,1664]{1,0:T(8,128)(2,1)}), bf16[1024,1664]{1,0:T(8,128)(2,1)}) %all-gather.8.cloned.1.call-update) | async-done | bytes 3407888 | tf_op jit(solution)/shard_map/all_gather | solution.py:488
  58.3 5.8 convolution_convert_fusion.4
  67.8 11.9 %piece_states.1 = (bf16[160,1024]{1,0:T(8,128)(2,1)}, bf16[160,128]{1,0:T(8,128)(2,1)}, bf16[3,160,1024]{2,1,0:T(8,128)(2,1)}, bf16[3,160,1024]{2,1,0:T(8,128)(2,1)}) custom-call(s32[1]{0:T(128)} %bitcast.1.flag_ref, f32[256,8]{1,0:T(8,128)} %constant.141.clone.tab_ref, bf16[256,1024]{1,0:T(8,128)(2,1)} %copy.69.kt_ref, bf16[1024,1024]{1,0:T(8,128)(2,1)} %slice.93.v_ref), custom_call_target="tpu_custom_call" | custom-call | flops 6442450944 | bytes 6291456 | tf_op jit(solution)/shard_map/piece_states/pallas_call | solution.py:361
  94.4 22.6 %all-gather.18.cloned.1.call-done = bf16[1280,1152]{1,0:T(8,128)(2,1)} async-done(((bf16[160,1152]{1,0:T(8,128)(2,1)}), bf16[1280,1152]{1,0:T(8,128)(2,1)}) %all-gather.18.cloned.1.call-update) | async-done | bytes 2949136 | tf_op jit(solution)/shard_map/all_gather | solution.py:567
  122.3 21.7 %attend_forward.1 = (bf16[1024,1024]{1,0:T(8,128)(2,1)}, f32[1024,1024]{1,0:T(8,128)}) custom-call(s32[1]{0:T(128)} %bitcast.1.flag_ref, f32[8,256]{1,0:T(8,128)} %constant.140.clone.tabr_ref, bf16[1024,256]{1,0:T(8,128)(2,1)} %get-tuple-element.119.q_ref, bf16[256,1024]{1,0:T(8,128)(2,1)} %copy.69.kt_ref, bf16[1024,1024]{1,0:T(8,128)(2,1)} %slice.93.v_ref, ...), custom_call_target="tpu_custom_call" | custom-call | flops 10737418240 | bytes 14680064 | tf_op jit(solution)/shard_map/attend_forward/pallas_call | solution.py:389
  153.9 53.5 %all-gather.14.cloned.1.call-done = bf16[1024,2752]{0,1:T(8,128)(2,1)} async-done(((bf16[128,2752]{0,1:T(8,128)(2,1)}), bf16[1024,2752]{0,1:T(8,128)(2,1)}) %all-gather.14.cloned.1.call-update) | async-done | bytes 5636112 | tf_op jit(solution)/shard_map/all_gather | solution.py:488
  207.5 11.3 %fusion.37 = f32[1024,2752]{0,1:T(8,128)} fusion(bf16[1024,2752]{0,1:T(8,128)(2,1)} %all-gather.14.cloned.1.call-done, bf16[1024,1024]{0,1:T(8,128)(2,1)S(1)} %multiply_convert_fusion.3), kind=kOutput, calls=%fused_computation.91 | convolution fusion | flops 5771362304 | bytes 19005440 | tf_op jit(solution)/shard_map/dot_general | solution.py:46
  218.8 48.1 %all-gather.12.cloned.1.call-done = bf16[1024,2752]{0,1:T(8,128)(2,1)} async-done(((bf16[128,2752]{0,1:T(8,128)(2,1)}), bf16[1024,2752]{0,1:T(8,128)(2,1)}) %all-gather.12.cloned.1.call-update) | async-done | bytes 5636112 | tf_op jit(solution)/shard_map/all_gather | solution.py:488
  266.8 11.5 %fusion.36 = f32[1024,2752]{0,1:T(8,128)} fusion(bf16[1024,2752]{0,1:T(8,128)(2,1)} %all-gather.12.cloned.1.call-done, bf16[1024,1024]{0,1:T(8,128)(2,1)} %copy-done.7), kind=kOutput, calls=%fused_computation.90 | convolution fusion | flops 5771362304 | bytes 19005440 | tf_op jit(solution)/shard_map/dot_general | solution.py:46
  278.4 47.9 %all-gather.16.cloned.1.call-done = bf16[1024,2752]{0,1:T(8,128)(2,1)} async-done(((bf16[128,2752]{0,1:T(8,128)(2,1)}), bf16[1024,2752]{0,1:T(8,128)(2,1)}) %all-gather.16.cloned.1.call-update) | async-done | bytes 5636112 | tf_op jit(solution)/shard_map/all_gather | solution.py:488
  326.2 20.0 %multiply_convert_fusion = (bf16[1024,2752]{0,1:T(8,128)(2,1)}, bf16[1024,2752]{0,1:T(8,128)(2,1)}, bf16[1024,2752]{0,1:T(8,128)(2,1)}) fusion(f32[1024,2752]{0,1:T(8,128)} %fusion.36, f32[1024,2752]{0,1:T(8,128)} %fusion.37, bf16[1024,1024]{1,0:T(8,128)(2,1)S(1)} %copy-done.6, bf16[1024,2752]{0,1:T(8,128)(2,1)} %all-gather.16.cloned.1.call-done), kind=kOutput, calls=%fused_computation | convolution fusion | flops 5816451072 | bytes 47185920 | tf_op jit(solution)/shard_map/dot_general | solution.py:46
  346.3 10.0 %fusion.35 = f32[1024,1024]{0,1:T(8,128)S(1)} fusion(bf16[1024,2752]{0,1:T(8,128)(2,1)} %get-tuple-element.114, bf16[1024,2752]{0,1:T(8,128)(2,1)} %all-gather.12.cloned.1.call-done), kind=kOutput, calls=%fused_computation.89 | convolution fusion | flops 5771362304 | bytes 15466496 | tf_op jit(solution)/shard_map/dot_general | solution.py:50
  356.3 9.1 %multiply_reduce_fusion = (bf16[1024]{0:T(1024)(128)(2,1)S(1)}, f32[1024]{0:T(1024)S(1)}, f32[1024,1024]{0,1:T(8,128)S(1)}) fusion(f32[1024,1024]{0,1:T(8,128)S(1)} %copy-done.3, f32[1024]{0:T(1024)S(1)} %add_rsqrt_fusion, f32[1024]{0:T(1024)S(1)} %get-tuple-element.102, f32[1024,1024]{0,1:T(8,128)S(1)} %fusion.35, bf16[1024,2752]{0,1:T(8,128)(2,1)S(1)} %copy-done.21, ...), kind=kOutput, calls=%fused_computation.25 | convolution fusion | flops 5778700288 | bytes 23869440 | tf_op jit(solution)/shard_map/dot_general | solution.py:50
  371.4 14.9 %state_gradients.1 = (bf16[1024,1024]{1,0:T(8,128)(2,1)}, bf16[1024,1024]{1,0:T(8,128)(2,1)}, bf16[2,160,1024]{2,1,0:T(8,128)(2,1)}, bf16[2,160,128]{2,1,0:T(8,1...) custom-call(s32[1]{0:T(128)} %bitcast.1.flag_ref, f32[256,8]{1,0:T(8,128)} %constant.141.clone.tab_ref, ...), custom_call_target="tpu_custom_call" | custom-call | flops 6442450944 | bytes 18874368 | tf_op jit(solution)/shard_map/state_gradients/pallas_call | solution.py:412
  390.9 10.3 %convolution_convert_fusion.2 = bf16[1024,2752]{0,1:T(8,128)(2,1)} fusion(bf16[1024,1024]{0,1:T(8,128)(2,1)} %copy-done.7, bf16[1024,2752]{0,1:T(8,128)(2,1)} %get-tuple-element.114), kind=kOutput, calls=%fused_computation.16 | convolution fusion | flops 5774180352 | bytes 13369344 | tf_op jit(solution)/shard_map/dot_general | solution.py:54
  401.2 8.4 %copy.87 = bf16[1024,2752]{1,0:T(8,128)(2,1)} copy(bf16[1024,2752]{0,1:T(8,128)(2,1)} %convolution_convert_fusion.2) | data formatting | bytes 11272192
  409.6 10.3 %convolution_convert_fusion.1 = bf16[1024,2752]{0,1:T(8,128)(2,1)} fusion(bf16[1024,1024]{0,1:T(8,128)(2,1)} %copy-done.7, bf16[1024,2752]{0,1:T(8,128)(2,1)} %get-tuple-element.113), kind=kOutput, calls=%fused_computation.15 | convolution fusion | flops 5774180352 | bytes 13369344 | tf_op jit(solution)/shard_map/dot_general | solution.py:54
  419.9 8.4 %copy.89 = bf16[1024,2752]{1,0:T(8,128)(2,1)} copy(bf16[1024,2752]{0,1:T(8,128)(2,1)} %convolution_convert_fusion.1) | data formatting | bytes 11272192
  428.3 10.6 %fusion.5 = bf16[1024,2752]{0,1:T(8,128)(2,1)} fusion(bf16[1024,2752]{0,1:T(8,128)(2,1)} %get-tuple-element.115, bf16[1024,1024]{1,0:T(8,128)(2,1)S(1)} %copy-done.6), kind=kOutput, calls=%fused_computation.17 | convolution fusion | flops 5774180352 | bytes 13369344 | tf_op jit(solution)/shard_map/dot_general | solution.py:54
  439.0 8.3 %copy.91 = bf16[1024,2752]{1,0:T(8,128)(2,1)} copy(bf16[1024,2752]{0,1:T(8,128)(2,1)} %fusion.5) | data formatting | bytes 11272192
  448.9 5.9 convolution_convert_fusion.5
  458.0 47.0 %attend_backward.1 = (bf16[1024,256]{1,0:T(8,128)(2,1)}, bf16[1024,256]{1,0:T(8,128)(2,1)}, bf16[1024,1024]{1,0:T(8,128)(2,1)}) custom-call(s32[1]{0:T(128)} %bitcast.1.flag_ref, f32[256,8]{1,0:T(8,128)} %constant.141.clone.tab_ref, f32[8,256]{1,0:T(8,128)} %constant.140.clone.tabr_ref, bf16[1024,256]{1,0:T(8,128)(2,1)} %get-tuple-element.119.q_ref, ...), custom_call_target="tpu_custom_call" | custom-call | flops 34359738368 | bytes 16777216 | tf_op jit(solution)/shard_map/attend_backward/pallas_call | solution.py:450
  509.7 5.2 fusion.11
  515.2 5.8 convolution_convert_fusion.3
  525.4 35.0 %reduce-scatter.21.cloned.1.call-done = bf16[128,2752]{1,0:T(8,128)(2,1)} async-done(((bf16[1024,2752]{1,0:T(8,128)(2,1)}), bf16[128,2752]{1,0:T(8,128)(2,1)}) %reduce-scatter.21.cloned.1.call-update) | async-done | bytes 704528
  562.7 63.2 %reduce-scatter.23.cloned.1.call-done = bf16[128,2752]{1,0:T(8,128)(2,1)} async-done(((bf16[1024,2752]{1,0:T(8,128)(2,1)}), bf16[128,2752]{1,0:T(8,128)(2,1)}) %reduce-scatter.23.cloned.1.call-update) | async-done | bytes 704528
  628.1 34.6 %reduce-scatter.17.cloned.1.call-done = bf16[128,1024]{1,0:T(8,128)(2,1)} async-done(((bf16[1024,1024]{1,0:T(8,128)(2,1)}), bf16[128,1024]{1,0:T(8,128)(2,1)}) %reduce-scatter.17.cloned.1.call-update) | async-done | bytes 262160 | tf_op jit(solution)/shard_map/reduce_scatter | solution.py:492
  662.7 43.2 %reduce-scatter.15.cloned.1.call-done = bf16[128,1664]{1,0:T(8,128)(2,1)} async-done(((bf16[1024,1664]{1,0:T(8,128)(2,1)}), bf16[128,1664]{1,0:T(8,128)(2,1)}) %reduce-scatter.15.cloned.1.call-update) | async-done | bytes 426000 | tf_op jit(solution)/shard_map/reduce_scatter | solution.py:492
  705.9 11.7 %add_convert_fusion = bf16[1024,1024]{0,1:T(8,128)(2,1)} fusion(f32[1024,1024]{0,1:T(8,128)} %copy-done.2, bf16[1024,2752]{0,1:T(8,128)(2,1)} %get-tuple-element.115, bf16[1024,2752]{0,1:T(8,128)(2,1)} %all-gather.16.cloned.1.call-done), kind=kOutput, calls=%fused_computation.28 | convolution fusion | flops 5773459456 | bytes 17563648 | tf_op jit(solution)/shard_map/dot_general | solution.py:50
  721.5 6.5 fusion.10
  728.1 5.4 copy.82
  733.5 57.5 %all-reduce.5.cloned.1.call-done = (bf16[128,1664]{1,0:T(8,128)(2,1)}, bf16[128,1024]{1,0:T(8,128)(2,1)}, bf16[128,2752]{0,1:T(8,128)(2,1)}, bf16[128,2752]{0,1:T(8,128)(2,1)}, bf16[128,2752]{0,1:T(8,128)(2,1)}) async-done(((bf16[128,1664]{1,0:T(8,128)(2,1)}, bf16[128,1024]{1,0:T(8,128)(2,1)}, bf16[128,2752]{0,1:T(8,128)(2,1)}, bf16[128,2752]{0,1:T(8,128)(2,1)}, bf16[128,2752]{0,1:T(8,128)(2,1)}), ...) | async-done | bytes 2801680 | tf_op jit(solution)/shard_map/psum | solution.py:493
  (132 shorter events, 85.8 us)
Async XLA Ops:
  7.2 8.8 %copy-start.18 = (s32[1,8]{1,0:T(1,128)S(1)}, s32[1,8]{1,0:T(1,128)}, u32[]{:S(2)}) copy-start(s32[1,8]{1,0:T(1,128)} %param.29) | copy-start | bytes 100
  7.2 49.1 %all-gather.8.cloned.1.call-start = ((), (), s32[]{:S(2)}) async-start(), calls=%async_computation.6 | async-start | bytes 3833856 | tf_op jit(solution)/shard_map/all_gather | solution.py:488
  13.1 104.0 %all-gather.18.cloned.1.call-start = ((), (), s32[]{:S(2)}) async-start(), calls=%async_computation.14 | async-start | bytes 3317760 | tf_op jit(solution)/shard_map/all_gather | solution.py:567
  16.0 130.9 %copy-start = (bf16[1024,1024]{0,1:T(8,128)(2,1)}, bf16[1024,1024]{0,1:T(8,128)(2,1)S(1)}, u32[]{:S(2)}) copy-start(bf16[1024,1024]{0,1:T(8,128)(2,1)S(1)} %copy.64) | copy-start | bytes 6291460
  17.8 39.8 %copy-start.15 = (f32[1024]{0:T(1024)}, f32[1024]{0:T(1024)S(1)}, u32[]{:S(2)}) copy-start(f32[1024]{0:T(1024)S(1)} %add_rsqrt_fusion.1) | copy-start | bytes 12292
  79.7 11.8 %copy-start.17 = (s32[1,8]{1,0:T(1,128)S(1)}, s32[1,8]{1,0:T(1,128)}, u32[]{:S(2)}) copy-start(s32[1,8]{1,0:T(1,128)} %param.30) | copy-start | bytes 100
  81.5 65.4 %all-gather.10.cloned.1.call-start = ((), (), s32[]{:S(2)}) async-start(), calls=%async_computation.7 | async-start | bytes 2359296 | tf_op jit(solution)/shard_map/all_gather | solution.py:488
  82.2 125.2 %all-gather.14.cloned.1.call-start = ((), (), s32[]{:S(2)}) async-start(), calls=%async_computation.9 | async-start | bytes 6340608 | tf_op jit(solution)/shard_map/all_gather | solution.py:488
  82.8 184.0 %all-gather.12.cloned.1.call-start = ((), (), s32[]{:S(2)}) async-start(), calls=%async_computation.8 | async-start | bytes 6340608 | tf_op jit(solution)/shard_map/all_gather | solution.py:488
  83.4 242.8 %all-gather.16.cloned.1.call-start = ((), (), s32[]{:S(2)}) async-start(), calls=%async_computation.10 | async-start | bytes 6340608 | tf_op jit(solution)/shard_map/all_gather | solution.py:488
  84.0 370.9 %reduce-scatter.13.cloned.1.call-start = ((), (), s32[]{:S(2)}) async-start(), calls=%async_computation.11 | async-start | bytes 3317760 | tf_op jit(solution)/shard_map/reduce_scatter | solution.py:608
  151.5 2.0 copy-start.2
  153.9 53.6 %copy-start.7 = (bf16[1024,1024]{0,1:T(8,128)(2,1)}, bf16[1024,1024]{0,1:T(8,128)(2,1)S(1)}, u32[]{:S(2)}) copy-start(bf16[1024,1024]{0,1:T(8,128)(2,1)S(1)} %multiply_convert_fusion.3) | copy-start | bytes 6291460
  218.8 107.5 %copy-start.6 = (bf16[1024,1024]{1,0:T(8,128)(2,1)S(1)}, bf16[1024,1024]{1,0:T(8,128)(2,1)}, u32[]{:S(2)}) copy-start(bf16[1024,1024]{1,0:T(8,128)(2,1)} %param.31) | copy-start | bytes 6291460
  346.3 10.0 %copy-start.3 = (f32[1024,1024]{0,1:T(8,128)S(1)}, f32[1024,1024]{0,1:T(8,128)}, u32[]{:S(2)}) copy-start(f32[1024,1024]{0,1:T(8,128)} %copy-done.2) | copy-start | bytes 12582916
  346.3 10.0 %copy-start.21 = (bf16[1024,2752]{0,1:T(8,128)(2,1)S(1)}, bf16[1024,2752]{0,1:T(8,128)(2,1)}, u32[]{:S(2)}) copy-start(bf16[1024,2752]{0,1:T(8,128)(2,1)} %get-tuple-element.113) | copy-start | bytes 16908292
  356.3 9.2 %copy-start.5 = (bf16[1024,1024]{0,1:T(8,128)(2,1)S(1)}, bf16[1024,1024]{0,1:T(8,128)(2,1)}, u32[]{:S(2)}) copy-start(bf16[1024,1024]{0,1:T(8,128)(2,1)} %copy.71) | copy-start | bytes 6291460
  367.1 4.4 copy-start.4
  390.8 132.4 %reduce-scatter.19.cloned.1.call-start = ((), (), s32[]{:S(2)}) async-start(), calls=%async_computation.15 | async-start | bytes 6488064
  409.5 150.9 %reduce-scatter.21.cloned.1.call-start = ((), (), s32[]{:S(2)}) async-start(), calls=%async_computation.16 | async-start | bytes 6488064
  428.3 197.6 %reduce-scatter.23.cloned.1.call-start = ((), (), s32[]{:S(2)}) async-start(), calls=%async_computation.17 | async-start | bytes 6488064
  447.3 215.4 %reduce-scatter.17.cloned.1.call-start = ((), (), s32[]{:S(2)}) async-start(), calls=%async_computation.13 | async-start | bytes 2359296 | tf_op jit(solution)/shard_map/reduce_scatter | solution.py:492
  454.8 251.0 %reduce-scatter.15.cloned.1.call-start = ((), (), s32[]{:S(2)}) async-start(), calls=%async_computation.12 | async-start | bytes 3833856 | tf_op jit(solution)/shard_map/reduce_scatter | solution.py:492
  505.0 4.7 copy-start.1
  505.0 4.7 copy-start.12
  505.0 4.7 copy-start.14
  505.0 4.7 copy-start.16
  509.7 5.3 copy-start.11
  523.1 267.9 %all-reduce.5.cloned.1.call-start = ((), (), s32[]{:S(2)}) async-start(), calls=%async_computation.18 | async-start | bytes 5603328 | tf_op jit(solution)/shard_map/psum | solution.py:493
  791.0 6.9 copy-start.9
  791.0 8.1 copy-start.8
  792.2 8.8 %copy-start.10 = (bf16[128,1024]{1,0:T(8,128)(2,1)S(1)}, bf16[128,1024]{1,0:T(8,128)(2,1)}, u32[]{:S(2)}) copy-start(bf16[128,1024]{1,0:T(8,128)(2,1)} %get-tuple-element.107) | copy-start | bytes 786436
  (3 other events, 3.8 us)
Sparse Core Ops, SparseCore 0:
  13.2 43.0 all-gather.7
  81.6 35.4 all-gather.17
  118.7 28.1 all-gather.9
  148.3 59.1 all-gather.13
  208.9 57.9 all-gather.11
  268.3 57.9 all-gather.15
  390.9 37.3 reduce-scatter.12
  430.6 64.2 reduce-scatter.18
  497.2 63.2 reduce-scatter.20
  562.6 63.2 reduce-scatter.22
  628.2 34.5 reduce-scatter.16
  664.9 40.9 reduce-scatter.14
  710.7 80.2 all-reduce.4
